TPU v7x, 128 devices: a whole 4x4x4 slice. The times are simulated.
128 devices in a mesh: dp: 8 (over x_hi, z), cent: 16 (over x_lo, y, core).
Axes of the slice: x: 4 (x_hi: 2, x_lo: 2; x = x_hi * 2 + x_lo), y: 4, z: 4, core: 2. Of those that a mesh axis runs over, the one named last changes fastest.
Arguments:
- points: bfloat16 [16384, 1024], P(('dp', 'cent')), may hold values from -6 to 6
- centroids: bfloat16 [32768, 1024], P('cent'), may hold values from -6 to 6
Outputs:
- centroids_next: float32 [1024, 32768], P('dp', 'cent')
All inputs are finite; a program needn't handle non-finite values.
Results may differ from a plain program's by a relative error of at most 0.007.
Values may be sent and summed in bfloat16 or wider, within the bound.
No kernel may reach another device: no remote copies, remote signals or barrier semaphores. Data moves between devices by JAX's collectives and lax.ppermute only.
A program may use at most 128 MiB of HBM per device.

v0:
```python
import jax
import jax.numpy as jnp
from jax import lax
from jax.sharding import PartitionSpec as P

BETA_GAIN = 4.0
PRIOR = 0.5


def local(points, centroids):
    features = points.shape[1]
    sharpness = BETA_GAIN * features ** (-0.5)
    gathered = lax.all_gather(points, "cent", axis=0, tiled=True)
    sqnorm = jnp.sum(jnp.square(centroids.astype(jnp.float32)), axis=1)
    total_rows = gathered.shape[0]
    block_rows = min(512, total_rows)
    blocks = gathered.reshape(total_rows // block_rows, block_rows, features)
    shard_cents = centroids.shape[0]

    def logits_of(xblock):
        dots = lax.dot_general(
            xblock, centroids, (((1,), (1,)), ((), ())), preferred_element_type=jnp.float32
        )
        return sharpness * (dots - 0.5 * sqnorm[None, :])

    def resp_of(logits, row_top, row_total):
        return (jnp.exp(logits - row_top[:, None]) / row_total[:, None]).astype(jnp.bfloat16)

    logits = lax.map(logits_of, blocks)
    local_max = jnp.max(logits, axis=-1)
    local_sum = jnp.sum(jnp.exp(logits - local_max[..., None]), axis=-1)
    row_top = lax.pmax(local_max, "cent")
    row_total = lax.psum(local_sum * jnp.exp(local_max - row_top), "cent")
    resp = jax.vmap(resp_of)(logits, row_top, row_total)
    resp = resp.reshape(total_rows, shard_cents)
    counts = jnp.sum(resp.astype(jnp.float32), axis=0)
    dp_count = lax.axis_size("dp")
    dp_index = lax.axis_index("dp")
    column_share = features // dp_count
    numer = lax.psum_scatter(
        lax.dot_general(
            gathered, resp, (((0,), (0,)), ((), ())), preferred_element_type=jnp.float32
        ).astype(jnp.bfloat16),
        "dp",
        scatter_dimension=0,
        tiled=True,
    ).astype(jnp.float32)
    counts_all = lax.psum(counts, "dp")
    own_cols = (
        lax.dynamic_slice_in_dim(centroids, dp_index * column_share, column_share, 1)
        .astype(jnp.float32)
        .T
    )
    result = (numer + PRIOR * own_cols) / (counts_all[None, :] + PRIOR)
    return result


def solution(mesh):
    return jax.shard_map(
        local,
        mesh=mesh,
        in_specs=(P(("dp", "cent"), None), P("cent", None)),
        out_specs=P("dp", "cent"),
        check_vma=False,
    )
```

profile of v0, /device:TPU:0, one launch (start us, length us, event | category | flops | bytes accessed | tf_op | source)
XLA Modules:
  0.0 268.6 jit_solution(6856425457871237441)
XLA Ops:
  6.5 0.0 all-gather.2.cloned.1.call-start
  6.5 0.7 all-gather.2.cloned.1.call-update
  7.3 0.0 reduce-scatter.4.cloned.1.call-start
  7.3 3.1 %multiply_reduce_fusion = f32[2048]{0:T(1024)S(1)} fusion(bf16[2048,1024]{1,0:T(8,128)(2,1)} %param.5), kind=kLoop, calls=%fused_computation.8 | loop fusion | flops 6289408 | bytes 4202496 | tf_op jit(solution)/shard_map/reduce_sum | solution.py:14
  10.4 38.5 %all-gather.2.cloned.1.call-done = bf16[2048,1024]{1,0:T(8,128)(2,1)} async-done(((bf16[128,1024]{1,0:T(8,128)(2,1)}), bf16[2048,1024]{1,0:T(8,128)(2,1)}) %all-gather.2.cloned.1.call-update) | async-done | bytes 4194320 | tf_op jit(solution)/shard_map/all_gather | solution.py:13
  48.9 27.4 %while.10 = (s32[]{:T(128)}, f32[4,512,2048]{2,1,0:T(8,128)}, bf16[4,512,1024]{2,1,0:T(8,128)(2,1)}, bf16[2048,1024]{1,0:T(8,128)(2,1)}, f32[2048]{0:T(1024)S(1)}, /*index=5*/s32[]{:T(128)}) while((s32[]{:T(128)}, f32[4,512,2048]{2,1,0:T(8,128)}, bf16[4,512,1024]{2,1,0:T(8,128)(2,1)}, bf16[2048,1024]{1,0:T(8,128)(2,1)}, f32[2048]{0:T(1024)S(1)}, ...), condition=%wide.region_2.3_spmd, body=%wide.region_1.2_spmd.sunk | while | flops 2149582848 | bytes 9462853 | solution.py:29
  48.9 6.8 %bitcast_dynamic-update-slice_fusion.2 = f32[4,512,2048]{2,1,0:T(8,128)} fusion(f32[4,512,2048]{2,1,0:T(8,128)} %get-tuple-element.83, s32[]{:T(128)} %get-tuple-element.82, bf16[2048,1024]{1,0:T(8,128)(2,1)} %get-tuple-element.91, f32[2048]{0:T(1024)S(1)} %broadcast_multiply_fusion.2, bf16[4,512,1024]{2,1,0:T(8,128)(2,1)} %get-tuple-element.90), kind=kOutput, calls=%fused_computation.clone.1 | convolution fusion | flops 2149580800 | bytes 9446400 | tf_op jit(solution)/shard_map/while/body/eval_jaxpr/dot_general | solution.py:21
  55.7 6.9 %bitcast_dynamic-update-slice_fusion.2 = f32[4,512,2048]{2,1,0:T(8,128)} fusion(f32[4,512,2048]{2,1,0:T(8,128)} %get-tuple-element.83, s32[]{:T(128)} %get-tuple-element.82, bf16[2048,1024]{1,0:T(8,128)(2,1)} %get-tuple-element.91, f32[2048]{0:T(1024)S(1)} %broadcast_multiply_fusion.2, bf16[4,512,1024]{2,1,0:T(8,128)(2,1)} %get-tuple-element.90), kind=kOutput, calls=%fused_computation.clone.1 | convolution fusion | flops 2149580800 | bytes 9446400 | tf_op jit(solution)/shard_map/while/body/eval_jaxpr/dot_general | solution.py:21
  62.6 6.9 %bitcast_dynamic-update-slice_fusion.2 = f32[4,512,2048]{2,1,0:T(8,128)} fusion(f32[4,512,2048]{2,1,0:T(8,128)} %get-tuple-element.83, s32[]{:T(128)} %get-tuple-element.82, bf16[2048,1024]{1,0:T(8,128)(2,1)} %get-tuple-element.91, f32[2048]{0:T(1024)S(1)} %broadcast_multiply_fusion.2, bf16[4,512,1024]{2,1,0:T(8,128)(2,1)} %get-tuple-element.90), kind=kOutput, calls=%fused_computation.clone.1 | convolution fusion | flops 2149580800 | bytes 9446400 | tf_op jit(solution)/shard_map/while/body/eval_jaxpr/dot_general | solution.py:21
  69.4 6.8 %bitcast_dynamic-update-slice_fusion.2 = f32[4,512,2048]{2,1,0:T(8,128)} fusion(f32[4,512,2048]{2,1,0:T(8,128)} %get-tuple-element.83, s32[]{:T(128)} %get-tuple-element.82, bf16[2048,1024]{1,0:T(8,128)(2,1)} %get-tuple-element.91, f32[2048]{0:T(1024)S(1)} %broadcast_multiply_fusion.2, bf16[4,512,1024]{2,1,0:T(8,128)(2,1)} %get-tuple-element.90), kind=kOutput, calls=%fused_computation.clone.1 | convolution fusion | flops 2149580800 | bytes 9446400 | tf_op jit(solution)/shard_map/while/body/eval_jaxpr/dot_general | solution.py:21
  76.3 6.6 %reduce_max.9 = f32[4,512]{1,0:T(4,128)S(1)} reduce(f32[4,512,2048]{2,1,0:T(8,128)} %get-tuple-element.32, f32[]{:T(128)} %constant.20.clone.1), dimensions={2}, to_apply=%region_3.4 | reduce | flops 4192256 | bytes 16785412 | tf_op jit(solution)/shard_map/reduce_max | solution.py:30
  82.9 8.1 %exponential_reduce_fusion = f32[4,512]{1,0:T(4,128)S(1)} fusion(f32[4,512,2048]{2,1,0:T(8,128)} %get-tuple-element.32, f32[4,512]{1,0:T(4,128)S(1)} %reduce_max.9), kind=kLoop, calls=%fused_computation.7 | loop fusion | flops 8386560 | bytes 16793600 | tf_op jit(solution)/shard_map/reduce_sum | solution.py:31
  91.0 29.7 %pmax.7 = f32[4,512]{1,0:T(4,128)S(1)} all-reduce(f32[4,512]{1,0:T(4,128)S(1)} %reduce_max.9), channel_id=1, replica_groups=mesh['dp'=8,'cent'=16] {'cent'}, use_global_device_ids=true, to_apply=%region_4.5 | all-reduce | flops 2048 | bytes 16384 | tf_op jit(solution)/shard_map/pmax | solution.py:32
  120.7 27.8 %psum.14 = f32[4,512]{1,0:T(4,128)S(1)} all-reduce(f32[4,512]{1,0:T(4,128)S(1)} %exponential_multiply_fusion), channel_id=1, replica_groups=mesh['dp'=8,'cent'=16] {'cent'}, use_global_device_ids=true, to_apply=%region_6.7 | all-reduce | flops 2048 | bytes 16384 | tf_op jit(solution)/shard_map/psum | solution.py:33
  148.5 0.0 copy-start
  148.5 8.0 %convert_reduce_fusion = (f32[2048]{0:T(1024)S(1)}, bf16[4,512,2048]{2,1,0:T(8,128)(2,1)S(1)}) fusion(f32[4,512]{1,0:T(4,128)S(1)} %psum.14, f32[4,512,2048]{2,1,0:T(8,128)} %get-tuple-element.32, f32[4,512]{1,0:T(4,128)S(1)} %pmax.7), kind=kLoop, calls=%fused_computation.5 | loop fusion | flops 20969472 | bytes 25190400 | tf_op jit(solution)/shard_map/reduce_sum | solution.py:36
  156.6 0.0 copy-done
  156.6 10.9 %convert_bitcast_fusion = bf16[1024,2048]{0,1:T(8,128)(2,1)} fusion(bf16[2048,2048]{1,0:T(8,128)(2,1)S(1)} %bitcast.23, bf16[2048,1024]{1,0:T(8,128)(2,1)S(1)} %bitcast.25), kind=kOutput, calls=%fused_computation.9 | convolution fusion | flops 8592031744 | bytes 16777216 | tf_op jit(solution)/shard_map/dot_general | solution.py:41
  167.5 6.5 %copy.5 = bf16[1024,2048]{1,0:T(8,128)(2,1)} copy(bf16[1024,2048]{0,1:T(8,128)(2,1)} %convert_bitcast_fusion) | data formatting | bytes 8388608
  174.0 0.0 reduce-scatter.4.cloned.1.call-update
  174.0 24.5 %psum.15 = f32[2048]{0:T(1024)S(1)} all-reduce(f32[2048]{0:T(1024)S(1)} %get-tuple-element.43), channel_id=1, replica_groups=mesh['dp'=8,'cent'=16] {'dp'}, use_global_device_ids=true, to_apply=%region_9.10 | all-reduce | flops 2048 | bytes 16384 | tf_op jit(solution)/shard_map/psum | solution.py:48
  198.6 59.1 %reduce-scatter.4.cloned.1.call-done = bf16[128,2048]{1,0:T(8,128)(2,1)} async-done(((bf16[1024,2048]{1,0:T(8,128)(2,1)}), bf16[128,2048]{1,0:T(8,128)(2,1)}) %reduce-scatter.4.cloned.1.call-update) | async-done | bytes 524304
  257.7 1.3 copy.6
  259.0 1.4 fusion.3
  260.4 1.3 copy.4
  (7 shorter events, 0.0 us)
Async XLA Ops:
  6.5 42.4 %all-gather.2.cloned.1.call-start = ((), (), s32[]{:S(2)}) async-start(), calls=%async_computation.1 | async-start | bytes 4456448 | tf_op jit(solution)/shard_map/all_gather | solution.py:13
  7.3 250.5 %reduce-scatter.4.cloned.1.call-start = ((), (), s32[]{:S(2)}) async-start(), calls=%async_computation.2 | async-start | bytes 4718592
  148.5 8.1 %copy-start = (bf16[4,512,1024]{2,1,0:T(8,128)(2,1)S(1)}, bf16[4,512,1024]{2,1,0:T(8,128)(2,1)}, u32[]{:S(2)}) copy-start(bf16[4,512,1024]{2,1,0:T(8,128)(2,1)} %get-tuple-element.103) | copy-start | bytes 12582916
Sparse Core Ops, SparseCore 0:
  9.1 39.8 all-gather.1
  174.1 83.5 reduce-scatter.3
where the time goes:
time: 269 us
  waiting for transfers between devices  98.4 us (37%)
  blocking collectives  82 us (30%)
  matrix products  38.3 us (14%)
  other arithmetic  27.2 us (10%)
  between operations  13.5 us (5%)
  local copies, waits for them, and re-layouts  9.11 us (3%)
    unnamed x3, waiting for transfers between devices  59.9 us
    all_gather x1, waiting for transfers between devices, local(): gathered = lax.all_gather(points, 'cent', axis=0, tiled=True)  38.5 us
    pmax x1, blocking collectives, local(): row_top = lax.pmax(local_max, 'cent')  29.7 us
    psum x1, blocking collectives, local(): row_total = lax.psum(local_sum * jnp.exp(local_max - row_top), 'cent')  27.8 us
    dot_general x4, matrix products, logits_of(): lax.dot_general(xblock, centroids, (((1,), (1,)), ((), ())), preferred_el...  27.4 us
    psum x1, blocking collectives, local(): counts_all = lax.psum(counts, 'dp')  24.5 us
    dot_general x1, matrix products, local(): lax.dot_general(gathered, resp, (((0,), (0,)), ((), ())), preferred_eleme...  10.9 us
    reduce_sum x1, other arithmetic, local(): local_sum = jnp.sum(jnp.exp(logits - local_max[..., None]), axis=-1)  8.12 us
  transfers between devices with their start and end apart: 2, of which 2 were waited for; matrix products, arithmetic and copies ran while one was open for 1% of the time, Pallas kernels for 0%

commit v1 on v0

--- a/solution.py
+++ b/solution.py
@@ -30,7 +30,7 @@
     local_max = jnp.max(logits, axis=-1)
     local_sum = jnp.sum(jnp.exp(logits - local_max[..., None]), axis=-1)
     row_top = lax.pmax(local_max, "cent")
-    row_total = lax.psum(local_sum * jnp.exp(local_max - row_top), "cent")
+    row_total = jnp.sum(lax.all_gather(local_sum * jnp.exp(local_max - row_top), "cent"), axis=0)
     resp = jax.vmap(resp_of)(logits, row_top, row_total)
     resp = resp.reshape(total_rows, shard_cents)
     counts = jnp.sum(resp.astype(jnp.float32), axis=0)

time: 269 us -> 259 us (0.963)
  blocking collectives: 82 us -> 70.9 us
    psum x1 -> x0, blocking collectives: 27.8 us -> none  [local(): row_total = lax.psum(local_sum * jnp.exp(local_max - row_top), 'cent')]
    all_gather x0 -> x1, blocking collectives: none -> 16.5 us  [local(): lax.all_gather(local_sum * jnp.exp(local_max - row_top), 'cent')]
where the time goes in v1:
time: 259 us; the launch traced here: 258 us
  waiting for transfers between devices  99.3 us (38%)
  blocking collectives  70.9 us (27%)
  matrix products  38.3 us (15%)
  other arithmetic  27.3 us (11%)
  between operations  13.5 us (5%)
  local copies, waits for them, and re-layouts  9.11 us (4%)
    unnamed x3, waiting for transfers between devices  60.8 us
    all_gather x1, waiting for transfers between devices, local(): gathered = lax.all_gather(points, 'cent', axis=0, tiled=True)  38.5 us
    pmax x1, blocking collectives, local(): row_top = lax.pmax(local_max, 'cent')  29.7 us
    dot_general x4, matrix products, logits_of(): lax.dot_general(xblock, centroids, (((1,), (1,)), ((), ())), preferred_el...  27.4 us
    psum x1, blocking collectives, local(): counts_all = lax.psum(counts, 'dp')  24.7 us
    all_gather x1, blocking collectives, local(): lax.all_gather(local_sum * jnp.exp(local_max - row_top), 'cent')  16.5 us
    dot_general x1, matrix products, local(): lax.dot_general(gathered, resp, (((0,), (0,)), ((), ())), preferred_eleme...  10.9 us
    reduce_sum x1, other arithmetic, local(): local_sum = jnp.sum(jnp.exp(logits - local_max[..., None]), axis=-1)  8.12 us
  transfers between devices with their start and end apart: 2, of which 2 were waited for; matrix products, arithmetic and copies ran while one was open for 1% of the time, Pallas kernels for 0%

profile of v1, /device:TPU:0, one launch (start us, length us, event | category | flops | bytes accessed | tf_op | source)
XLA Modules:
  0.0 258.3 jit_solution(17266180986873743466)
XLA Ops:
  6.5 0.0 all-gather.4.cloned.1.call-start
  6.5 0.7 all-gather.4.cloned.1.call-update
  7.3 0.0 reduce-scatter.4.cloned.1.call-start
  7.3 3.1 %multiply_reduce_fusion = f32[2048]{0:T(1024)S(1)} fusion(bf16[2048,1024]{1,0:T(8,128)(2,1)} %param.5), kind=kLoop, calls=%fused_computation.8 | loop fusion | flops 6289408 | bytes 4202496 | tf_op jit(solution)/shard_map/reduce_sum | solution.py:14
  10.4 38.5 %all-gather.4.cloned.1.call-done = bf16[2048,1024]{1,0:T(8,128)(2,1)} async-done(((bf16[128,1024]{1,0:T(8,128)(2,1)}), bf16[2048,1024]{1,0:T(8,128)(2,1)}) %all-gather.4.cloned.1.call-update) | async-done | bytes 4194320 | tf_op jit(solution)/shard_map/all_gather | solution.py:13
  48.9 27.4 %while.10 = (s32[]{:T(128)}, f32[4,512,2048]{2,1,0:T(8,128)}, bf16[4,512,1024]{2,1,0:T(8,128)(2,1)}, bf16[2048,1024]{1,0:T(8,128)(2,1)}, f32[2048]{0:T(1024)S(1)}, /*index=5*/s32[]{:T(128)}) while((s32[]{:T(128)}, f32[4,512,2048]{2,1,0:T(8,128)}, bf16[4,512,1024]{2,1,0:T(8,128)(2,1)}, bf16[2048,1024]{1,0:T(8,128)(2,1)}, f32[2048]{0:T(1024)S(1)}, ...), condition=%wide.region_2.3_spmd, body=%wide.region_1.2_spmd.sunk | while | flops 2149582848 | bytes 9462853 | solution.py:29
  48.9 6.8 %bitcast_dynamic-update-slice_fusion.2 = f32[4,512,2048]{2,1,0:T(8,128)} fusion(f32[4,512,2048]{2,1,0:T(8,128)} %get-tuple-element.83, s32[]{:T(128)} %get-tuple-element.82, bf16[2048,1024]{1,0:T(8,128)(2,1)} %get-tuple-element.91, f32[2048]{0:T(1024)S(1)} %broadcast_multiply_fusion.2, bf16[4,512,1024]{2,1,0:T(8,128)(2,1)} %get-tuple-element.90), kind=kOutput, calls=%fused_computation.clone.1 | convolution fusion | flops 2149580800 | bytes 9446400 | tf_op jit(solution)/shard_map/while/body/eval_jaxpr/dot_general | solution.py:21
  55.7 6.9 %bitcast_dynamic-update-slice_fusion.2 = f32[4,512,2048]{2,1,0:T(8,128)} fusion(f32[4,512,2048]{2,1,0:T(8,128)} %get-tuple-element.83, s32[]{:T(128)} %get-tuple-element.82, bf16[2048,1024]{1,0:T(8,128)(2,1)} %get-tuple-element.91, f32[2048]{0:T(1024)S(1)} %broadcast_multiply_fusion.2, bf16[4,512,1024]{2,1,0:T(8,128)(2,1)} %get-tuple-element.90), kind=kOutput, calls=%fused_computation.clone.1 | convolution fusion | flops 2149580800 | bytes 9446400 | tf_op jit(solution)/shard_map/while/body/eval_jaxpr/dot_general | solution.py:21
  62.6 6.9 %bitcast_dynamic-update-slice_fusion.2 = f32[4,512,2048]{2,1,0:T(8,128)} fusion(f32[4,512,2048]{2,1,0:T(8,128)} %get-tuple-element.83, s32[]{:T(128)} %get-tuple-element.82, bf16[2048,1024]{1,0:T(8,128)(2,1)} %get-tuple-element.91, f32[2048]{0:T(1024)S(1)} %broadcast_multiply_fusion.2, bf16[4,512,1024]{2,1,0:T(8,128)(2,1)} %get-tuple-element.90), kind=kOutput, calls=%fused_computation.clone.1 | convolution fusion | flops 2149580800 | bytes 9446400 | tf_op jit(solution)/shard_map/while/body/eval_jaxpr/dot_general | solution.py:21
  69.4 6.8 %bitcast_dynamic-update-slice_fusion.2 = f32[4,512,2048]{2,1,0:T(8,128)} fusion(f32[4,512,2048]{2,1,0:T(8,128)} %get-tuple-element.83, s32[]{:T(128)} %get-tuple-element.82, bf16[2048,1024]{1,0:T(8,128)(2,1)} %get-tuple-element.91, f32[2048]{0:T(1024)S(1)} %broadcast_multiply_fusion.2, bf16[4,512,1024]{2,1,0:T(8,128)(2,1)} %get-tuple-element.90), kind=kOutput, calls=%fused_computation.clone.1 | convolution fusion | flops 2149580800 | bytes 9446400 | tf_op jit(solution)/shard_map/while/body/eval_jaxpr/dot_general | solution.py:21
  76.3 6.6 %reduce_max.9 = f32[4,512]{1,0:T(4,128)S(1)} reduce(f32[4,512,2048]{2,1,0:T(8,128)} %get-tuple-element.32, f32[]{:T(128)} %constant.20.clone.1), dimensions={2}, to_apply=%region_3.4 | reduce | flops 4192256 | bytes 16785412 | tf_op jit(solution)/shard_map/reduce_max | solution.py:30
  82.9 8.1 %exponential_reduce_fusion = f32[4,512]{1,0:T(4,128)S(1)} fusion(f32[4,512,2048]{2,1,0:T(8,128)} %get-tuple-element.32, f32[4,512]{1,0:T(4,128)S(1)} %reduce_max.9), kind=kLoop, calls=%fused_computation.7 | loop fusion | flops 8386560 | bytes 16793600 | tf_op jit(solution)/shard_map/reduce_sum | solution.py:31
  91.0 29.7 %pmax.7 = f32[4,512]{1,0:T(4,128)S(1)} all-reduce(f32[4,512]{1,0:T(4,128)S(1)} %reduce_max.9), channel_id=1, replica_groups=mesh['dp'=8,'cent'=16] {'cent'}, use_global_device_ids=true, to_apply=%region_4.5 | all-reduce | flops 2048 | bytes 16384 | tf_op jit(solution)/shard_map/pmax | solution.py:32
  120.7 16.5 %all-gather.1 = f32[16,4,512]{2,1,0:T(4,128)S(1)} all-gather(f32[1,4,512]{2,1,0:T(4,128)S(1)} %multiply_bitcast_fusion), channel_id=2, replica_groups=mesh['dp'=8,'cent'=16] {'cent'}, dimensions={0}, use_global_device_ids=true | all-gather | bytes 139264 | tf_op jit(solution)/shard_map/all_gather | solution.py:33
  137.2 0.0 copy-start
  137.2 8.0 %convert_reduce_fusion = (f32[2048]{0:T(1024)S(1)}, bf16[4,512,2048]{2,1,0:T(8,128)(2,1)S(1)}) fusion(f32[4,512]{1,0:T(4,128)S(1)} %reduce_sum.38, f32[4,512,2048]{2,1,0:T(8,128)} %get-tuple-element.32, f32[4,512]{1,0:T(4,128)S(1)} %pmax.7), kind=kLoop, calls=%fused_computation.5 | loop fusion | flops 20969472 | bytes 25190400 | tf_op jit(solution)/shard_map/reduce_sum | solution.py:36
  145.2 0.0 copy-done
  145.3 10.9 %convert_bitcast_fusion = bf16[1024,2048]{0,1:T(8,128)(2,1)} fusion(bf16[2048,2048]{1,0:T(8,128)(2,1)S(1)} %bitcast.25, bf16[2048,1024]{1,0:T(8,128)(2,1)S(1)} %bitcast.27), kind=kOutput, calls=%fused_computation.9 | convolution fusion | flops 8592031744 | bytes 16777216 | tf_op jit(solution)/shard_map/dot_general | solution.py:41
  156.2 6.5 %copy.5 = bf16[1024,2048]{1,0:T(8,128)(2,1)} copy(bf16[1024,2048]{0,1:T(8,128)(2,1)} %convert_bitcast_fusion) | data formatting | bytes 8388608
  162.7 0.0 reduce-scatter.4.cloned.1.call-update
  162.7 24.7 %psum.7 = f32[2048]{0:T(1024)S(1)} all-reduce(f32[2048]{0:T(1024)S(1)} %get-tuple-element.43), channel_id=1, replica_groups=mesh['dp'=8,'cent'=16] {'dp'}, use_global_device_ids=true, to_apply=%region_9.10 | all-reduce | flops 2048 | bytes 16384 | tf_op jit(solution)/shard_map/psum | solution.py:48
  187.4 60.0 %reduce-scatter.4.cloned.1.call-done = bf16[128,2048]{1,0:T(8,128)(2,1)} async-done(((bf16[1024,2048]{1,0:T(8,128)(2,1)}), bf16[128,2048]{1,0:T(8,128)(2,1)}) %reduce-scatter.4.cloned.1.call-update) | async-done | bytes 524304
  247.5 1.3 copy.6
  248.8 1.4 fusion.3
  250.2 1.3 copy.4
  (8 shorter events, 0.1 us)
Async XLA Ops:
  6.5 42.4 %all-gather.4.cloned.1.call-start = ((), (), s32[]{:S(2)}) async-start(), calls=%async_computation.1 | async-start | bytes 4456448 | tf_op jit(solution)/shard_map/all_gather | solution.py:13
  7.3 240.2 %reduce-scatter.4.cloned.1.call-start = ((), (), s32[]{:S(2)}) async-start(), calls=%async_computation.2 | async-start | bytes 4718592
  137.2 8.1 %copy-start = (bf16[4,512,1024]{2,1,0:T(8,128)(2,1)S(1)}, bf16[4,512,1024]{2,1,0:T(8,128)(2,1)}, u32[]{:S(2)}) copy-start(bf16[4,512,1024]{2,1,0:T(8,128)(2,1)} %get-tuple-element.103) | copy-start | bytes 12582916
Sparse Core Ops, SparseCore 0:
  9.1 39.8 all-gather.3
  162.8 84.6 reduce-scatter.3
